TPU v7x, 32 devices: a whole 2x2x4 slice. The times are simulated.
32 devices in a mesh: section: 4 (over y, x), dp: 8 (over z, core).
Axes of the slice: x: 2, y: 2, z: 4, core: 2. Of those that a mesh axis runs over, the one named last changes fastest.
Arguments:
- images: bfloat16 [4, 8, 8, 16, 768], P(None, 'dp'), may hold values from -6 to 6
- widths: int32 [4], replicated, may hold values from 0 to 2, as said below
- depth_kernel: bfloat16 [4, 7, 7, 768], P('section'), may hold values from -0.875 to 0.875
- depth_bias: bfloat16 [4, 768], P('section'), may hold values from -3 to 3
- ln_gain: bfloat16 [4, 768], P('section'), may hold values from 0.25 to 1.75
- ln_bias: bfloat16 [4, 768], P('section'), may hold values from -3 to 3
- w_in: bfloat16 [4, 1536, 768], P('section', 'dp'), may hold values from -0.21875 to 0.21875
- w_out: bfloat16 [4, 1536, 768], P('section', 'dp'), may hold values from -0.15625 to 0.15625
- layer_scale: bfloat16 [4, 768], P('section'), may hold values from 0.29882812 to 1
Outputs:
- section_acts: bfloat16 [4, 4, 8, 8, 16, 768], P('section', None, 'dp')
Inputs may be any that keep to these rules, and one draw needn't show every extreme that they name: `widths`: each half of the micro-batches holds exactly one at level 0 and one at a level above 0; levels 1 and 2 both appear.
All inputs are finite; a program needn't handle non-finite values.
Results may differ from a plain program's by a relative error of at most 0.0065.
Values may be sent and summed in bfloat16 or wider, within the bound.
A program may use at most 64 MiB of HBM per device.

v0:
```python
import jax
import jax.numpy as jnp
from jax import lax
from jax.sharding import PartitionSpec as P


def swapped(value, axis, stride):
    mask = 2**stride
    pairs = [(source, source ^ mask) for source in range(lax.axis_size(axis))]
    return lax.ppermute(value, axis, pairs)


def passed_along(value, axis, steps):
    count = lax.axis_size(axis)
    initial, last = (max(0, -steps), min(count, count - steps))
    return lax.ppermute(value, axis, [(source, source + steps) for source in range(initial, last)])


def conv_block(
    inputs, width_level, depth_kernel, depth_bias, ln_gain, ln_bias, w_in, w_out, layer_scale
):
    channels = inputs.shape[-1]
    hidden = w_in.shape[0]
    active_channels = jnp.where(
        width_level == 0, channels, jnp.where(width_level == 1, channels // 2, channels // 4)
    )
    active_hidden = jnp.where(
        width_level == 0, hidden, jnp.where(width_level == 1, hidden // 2, hidden // 4)
    )
    chan_mask = (jnp.arange(channels) < active_channels).astype(jnp.float32)
    hidden_mask = (jnp.arange(hidden) < active_hidden).astype(jnp.float32)
    channel_count = active_channels.astype(jnp.float32)
    widened = inputs.astype(jnp.float32) * chan_mask
    kernel = depth_kernel.astype(jnp.float32)
    reach = kernel.shape[0] // 2
    padded = jnp.pad(widened, ((0, 0), (reach, reach), (reach, reach), (0, 0)))
    rows_n = inputs.shape[1]
    cols_n = inputs.shape[2]
    spatial = jnp.zeros(widened.shape, jnp.float32)
    for row_off in range(kernel.shape[0]):
        for col_off in range(kernel.shape[1]):
            spatial = (
                spatial
                + padded[:, row_off : row_off + rows_n, col_off : col_off + cols_n, :]
                * kernel[row_off, col_off]
            )
    spatial = (spatial + depth_bias.astype(jnp.float32)) * chan_mask
    average = jnp.sum(spatial, axis=-1, keepdims=True) / channel_count
    centred = (spatial - average) * chan_mask
    variance = jnp.sum(centred * centred, axis=-1, keepdims=True) / channel_count
    normed = (
        centred * lax.rsqrt(variance + 1e-06) * ln_gain.astype(jnp.float32)
        + ln_bias.astype(jnp.float32)
    ) * chan_mask
    flattened = normed.astype(jnp.bfloat16).reshape(-1, channels)
    expanded = jnp.dot(flattened, w_in.T, preferred_element_type=jnp.float32)
    activated = (jax.nn.gelu(expanded, approximate=True) * hidden_mask).astype(jnp.bfloat16)
    projected = jnp.dot(activated, w_out, preferred_element_type=jnp.float32).reshape(widened.shape)
    result = widened + layer_scale.astype(jnp.float32) * projected * chan_mask
    return result.astype(jnp.bfloat16)


def run_slot(
    stored, received, tick_index, offset, entry_first, base_slot, count, images, widths, parameters
):
    slot_index = tick_index - offset
    is_live = (slot_index >= 0) & (slot_index < count)
    clipped = jnp.clip(slot_index, 0, count - 1) + base_slot
    entering = lax.dynamic_index_in_dim(images, clipped, 0, keepdims=False)
    source = jnp.where(entry_first, entering, received)
    width_level = widths[clipped]
    result = lax.cond(
        is_live,
        lambda operand: conv_block(operand, width_level, *parameters),
        lambda operand: jnp.zeros_like(operand),
        source,
    )
    previous = lax.dynamic_index_in_dim(stored, clipped, 0, keepdims=False)
    stored = lax.dynamic_update_index_in_dim(
        stored, jnp.where(is_live, result, previous), clipped, 0
    )
    return (stored, result)


def on_device(images, widths, depth_kernel, depth_bias, ln_gain, ln_bias, w_in, w_out, layer_scale):
    sections = lax.axis_size("section")
    position = lax.axis_index("section")
    microbatches = images.shape[0]
    halfway = microbatches // 2
    bit_total = sections.bit_length() - 1
    stored = jnp.zeros(images.shape, jnp.bfloat16)
    empty_tile = jnp.zeros(images.shape[1:], jnp.bfloat16)
    shards = (w_in, w_out, depth_kernel, depth_bias, ln_gain, ln_bias, layer_scale)
    for bit_index in range(bit_total):
        shards = swapped(
            (shards[0], shards[1], shards[2], shards[3], shards[4], shards[5], shards[6]),
            "section",
            bit_index,
        )
    full_in, full_out, mirror_in, mirror_out = (
        lax.all_gather(w_in, "dp", axis=1, tiled=True),
        lax.all_gather(w_out, "dp", axis=1, tiled=True),
        lax.all_gather(shards[0], "dp", axis=1, tiled=True),
        lax.all_gather(shards[1], "dp", axis=1, tiled=True),
    )
    own_params = (
        depth_kernel[0],
        depth_bias[0],
        ln_gain[0],
        ln_bias[0],
        full_in[0],
        full_out[0],
        layer_scale[0],
    )
    mirror_params = (
        shards[2][0],
        shards[3][0],
        shards[4][0],
        shards[5][0],
        mirror_in[0],
        mirror_out[0],
        shards[6][0],
    )
    tick_total = sections - 1 + halfway

    def advance(tick_index, carried):
        down_received, up_received, kept = carried
        kept, down_result = run_slot(
            kept,
            down_received,
            tick_index,
            position,
            position == 0,
            0,
            halfway,
            images,
            widths,
            own_params,
        )
        kept, up_result = run_slot(
            kept,
            up_received,
            tick_index,
            sections - 1 - position,
            position == sections - 1,
            halfway,
            halfway,
            images,
            widths,
            mirror_params,
        )
        down_received = passed_along(down_result, "section", 1)
        up_received = passed_along(up_result, "section", -1)
        return (down_received, up_received, kept)

    _, _, stored = lax.fori_loop(0, tick_total, advance, (empty_tile, empty_tile, stored))
    return stored[None]


def solution(mesh):
    placed = (
        P(None, "dp", None, None, None),
        P(),
        P("section", None, None, None),
        P("section", None),
        P("section", None),
        P("section", None),
        P("section", "dp", None),
        P("section", "dp", None),
        P("section", None),
    )
    return jax.shard_map(
        on_device,
        mesh=mesh,
        in_specs=placed,
        out_specs=P("section", None, "dp", None, None, None),
        check_vma=False,
    )
```

profile of v0, /device:TPU:6, one launch (start us, length us, event | category | flops | bytes accessed | tf_op | source)
XLA Modules:
  0.0 269.6 jit_solution(6992223651188118496)
XLA Ops:
  8.7 8.4 %collective-permute-done.12 = bf16[1,192,768]{2,1,0:T(8,128)(2,1)S(1)} collective-permute-done((bf16[1,192,768]{2,1,0:T(8,128)(2,1)}, bf16[1,192,768]{2,1,0:T(8,128)(2,1)S(1)}, u32[]{:S(2)}, u32[]{:S(2)}) %collective-permute-start.12) | collective-permute-done | bytes 294944 | tf_op jit(solution)/shard_map/ppermute | solution.py:10
  17.6 7.4 %collective-permute-done.13 = bf16[1,192,768]{2,1,0:T(8,128)(2,1)S(1)} collective-permute-done((bf16[1,192,768]{2,1,0:T(8,128)(2,1)S(1)}, bf16[1,192,768]{2,1,0:T(8,128)(2,1)S(1)}, u32[]{:S(2)}, u32[]{:S(2)}) %collective-permute-start.13) | collective-permute-done | bytes 294944 | tf_op jit(solution)/shard_map/ppermute | solution.py:10
  26.4 6.8 %collective-permute-done.14 = bf16[1,192,768]{2,1,0:T(8,128)(2,1)S(1)} collective-permute-done((bf16[1,192,768]{2,1,0:T(8,128)(2,1)}, bf16[1,192,768]{2,1,0:T(8,128)(2,1)S(1)}, u32[]{:S(2)}, u32[]{:S(2)}) %collective-permute-start.14) | collective-permute-done | bytes 294944 | tf_op jit(solution)/shard_map/ppermute | solution.py:10
  33.7 6.2 %collective-permute-done.15 = bf16[1,192,768]{2,1,0:T(8,128)(2,1)S(1)} collective-permute-done((bf16[1,192,768]{2,1,0:T(8,128)(2,1)S(1)}, bf16[1,192,768]{2,1,0:T(8,128)(2,1)S(1)}, u32[]{:S(2)}, u32[]{:S(2)}) %collective-permute-start.15) | collective-permute-done | bytes 294944 | tf_op jit(solution)/shard_map/ppermute | solution.py:10
  41.2 4.2 %collective-permute-done.4 = bf16[1,7,7,768]{3,2,1,0:T(8,128)(2,1)S(1)} collective-permute-done((bf16[1,7,7,768]{3,2,1,0:T(8,128)(2,1)}, bf16[1,7,7,768]{3,2,1,0:T(8,128)(2,1)S(1)}, u32[]{:S(2)}, u32[]{:S(2)}) %collective-permute-start.4) | collective-permute-done | bytes 75296 | tf_op jit(solution)/shard_map/ppermute | solution.py:10
  57.2 16.8 %all-gather.7.cloned.1.call-done = bf16[1,1536,768]{2,1,0:T(8,128)(2,1)} async-done(((bf16[1,192,768]{2,1,0:T(8,128)(2,1)}), bf16[1,1536,768]{2,1,0:T(8,128)(2,1)}) %all-gather.7.cloned.1.call-update) | async-done | bytes 2359312 | tf_op jit(solution)/shard_map/all_gather | solution.py:102
  74.0 32.4 %all-gather.9.cloned.1.call-done = bf16[1,1536,768]{2,1,0:T(8,128)(2,1)} async-done(((bf16[1,192,768]{2,1,0:T(8,128)(2,1)}), bf16[1,1536,768]{2,1,0:T(8,128)(2,1)}) %all-gather.9.cloned.1.call-update) | async-done | bytes 2359312 | tf_op jit(solution)/shard_map/all_gather | solution.py:103
  106.4 32.2 %all-gather.11.cloned.1.call-done = bf16[1,1536,768]{2,1,0:T(8,128)(2,1)} async-done(((bf16[1,192,768]{2,1,0:T(8,128)(2,1)}), bf16[1,1536,768]{2,1,0:T(8,128)(2,1)}) %all-gather.11.cloned.1.call-update) | async-done | bytes 2359312 | tf_op jit(solution)/shard_map/all_gather | solution.py:104
  138.7 123.5 %while.19 = (s32[]{:T(128)}, bf16[1,8,16,768]{3,2,1,0:T(8,128)(2,1)S(1)}, bf16[1,8,16,768]{3,2,1,0:T(8,128)(2,1)S(1)}, bf16[4,1,8,16,768]{4,3,2,1,0:T(8,128)(2,1...) while((s32[]{:T(128)}, ...), condition=%wide.region_9.10_spmd, body=%wide.region_0.9_spmd.sunk | while | flops 1235378944 | bytes 22721452 | solution.py:156
  138.8 10.3 %conditional.5 = (bf16[1,8,16,768]{3,2,1,0:T(8,128)(2,1)S(1)}) conditional(s32[]{:T(128)} %convert_element_type.176, () %tuple.160, (pred[]{:T(512)}, bf16[4,1,8,16,768]{4,3,2,1,0:T(8,128)(2,1)S(1)}, s32[]{:T(128)}, bf16[1,8,16,768]{3,2,1,0:T(8,128)(2,1)S(1)}, s32[4]{0:T(128)S(1)}, /*index=5*/bf16[768]{0:T(1024)(128)(2,1)S(1)}, ...), branch_computations={%region_5.5_spmd, %region_6.8_spmd} | conditional | flops 617591168 | bytes 9590903 | solution.py:72
  145.3 3.7 %fusion.129 = f32[128,768]{1,0:T(8,128)S(1)} fusion(bf16[1536,768]{1,0:T(8,128)(2,1)} %get-tuple-element.690, f32[1536]{0:T(1024)S(1)} %fusion.234, bf16[128,768]{1,0:T(8,128)(2,1)S(1)} %bitcast.51, bf16[1536,768]{1,0:T(8,128)(2,1)} %get-tuple-element.689), kind=kOutput, calls=%fused_computation.285 | convolution fusion | flops 605945856 | bytes 5314560 | tf_op jit(solution)/shard_map/while/body/eval_jaxpr/cond/branch_1_fun/dot_general | solution.py:58
  155.1 4.2 %collective-permute-done = bf16[1,8,16,768]{3,2,1,0:T(8,128)(2,1)S(1)} collective-permute-done((bf16[1,8,16,768]{3,2,1,0:T(8,128)(2,1)S(1)}, bf16[1,8,16,768]{3,2,1,0:T(8,128)(2,1)S(1)}, u32[]{:S(2)}, u32[]{:S(2)}) %collective-permute-start) | collective-permute-done | bytes 196640 | tf_op jit(solution)/shard_map/while/body/eval_jaxpr/ppermute | solution.py:16
  159.3 10.2 %conditional.5 = (bf16[1,8,16,768]{3,2,1,0:T(8,128)(2,1)S(1)}) conditional(s32[]{:T(128)} %convert_element_type.176, () %tuple.160, (pred[]{:T(512)}, bf16[4,1,8,16,768]{4,3,2,1,0:T(8,128)(2,1)S(1)}, s32[]{:T(128)}, bf16[1,8,16,768]{3,2,1,0:T(8,128)(2,1)S(1)}, s32[4]{0:T(128)S(1)}, /*index=5*/bf16[768]{0:T(1024)(128)(2,1)S(1)}, ...), branch_computations={%region_5.5_spmd, %region_6.8_spmd} | conditional | flops 617591168 | bytes 9590903 | solution.py:72
  174.8 4.8 %collective-permute-done = bf16[1,8,16,768]{3,2,1,0:T(8,128)(2,1)S(1)} collective-permute-done((bf16[1,8,16,768]{3,2,1,0:T(8,128)(2,1)S(1)}, bf16[1,8,16,768]{3,2,1,0:T(8,128)(2,1)S(1)}, u32[]{:S(2)}, u32[]{:S(2)}) %collective-permute-start) | collective-permute-done | bytes 196640 | tf_op jit(solution)/shard_map/while/body/eval_jaxpr/ppermute | solution.py:16
  179.7 12.5 %collective-permute-start.1 = (bf16[1,8,16,768]{3,2,1,0:T(8,128)(2,1)S(1)}, bf16[1,8,16,768]{3,2,1,0:T(8,128)(2,1)S(1)}, u32[]{:S(2)}, u32[]{:S(2)}) collective-permute-start(bf16[1,8,16,768]{3,2,1,0:T(8,128)(2,1)S(1)} %get-tuple-element.1098), channel_id=1, source_target_pairs={{8,0},{16,8},{24,16},{9,1},{17,9},{25,17},{10,2},{18,10},{26,18},{... | collective-permute-start | bytes 589832 | tf_op jit(solution)/shard_map/while/body/eval_jaxpr/ppermute | solution.py:16
  195.4 12.6 %collective-permute-done = bf16[1,8,16,768]{3,2,1,0:T(8,128)(2,1)S(1)} collective-permute-done((bf16[1,8,16,768]{3,2,1,0:T(8,128)(2,1)S(1)}, bf16[1,8,16,768]{3,2,1,0:T(8,128)(2,1)S(1)}, u32[]{:S(2)}, u32[]{:S(2)}) %collective-permute-start) | collective-permute-done | bytes 196640 | tf_op jit(solution)/shard_map/while/body/eval_jaxpr/ppermute | solution.py:16
  208.0 4.8 %collective-permute-start.1 = (bf16[1,8,16,768]{3,2,1,0:T(8,128)(2,1)S(1)}, bf16[1,8,16,768]{3,2,1,0:T(8,128)(2,1)S(1)}, u32[]{:S(2)}, u32[]{:S(2)}) collective-permute-start(bf16[1,8,16,768]{3,2,1,0:T(8,128)(2,1)S(1)} %get-tuple-element.1098), channel_id=1, source_target_pairs={{8,0},{16,8},{24,16},{9,1},{17,9},{25,17},{10,2},{18,10},{26,18},{... | collective-permute-start | bytes 589832 | tf_op jit(solution)/shard_map/while/body/eval_jaxpr/ppermute | solution.py:16
  212.9 10.2 %conditional.4 = (bf16[1,8,16,768]{3,2,1,0:T(8,128)(2,1)S(1)}) conditional(s32[]{:T(128)} %convert_element_type.175, () %tuple.158, (pred[]{:T(512)}, bf16[4,1,8,16,768]{4,3,2,1,0:T(8,128)(2,1)S(1)}, s32[]{:T(128)}, bf16[1,8,16,768]{3,2,1,0:T(8,128)(2,1)S(1)}, s32[4]{0:T(128)S(1)}, /*index=5*/bf16[768]{0:T(1024)(128)(2,1)S(1)}, ...), branch_computations={%region_1.1_spmd, %region_2.4_spmd} | conditional | flops 617591168 | bytes 9590903 | solution.py:72
  219.3 3.7 %fusion.9 = f32[128,768]{1,0:T(8,128)S(1)} fusion(bf16[1536,768]{1,0:T(8,128)(2,1)} %get-tuple-element.678, f32[1536]{0:T(1024)S(1)} %fusion.114, bf16[128,768]{1,0:T(8,128)(2,1)S(1)} %bitcast.52, bf16[1536,768]{1,0:T(8,128)(2,1)} %get-tuple-element.677), kind=kOutput, calls=%fused_computation.58 | convolution fusion | flops 605945856 | bytes 5314560 | tf_op jit(solution)/shard_map/while/body/eval_jaxpr/cond/branch_1_fun/dot_general | solution.py:58
  224.6 13.8 %collective-permute-done = bf16[1,8,16,768]{3,2,1,0:T(8,128)(2,1)S(1)} collective-permute-done((bf16[1,8,16,768]{3,2,1,0:T(8,128)(2,1)S(1)}, bf16[1,8,16,768]{3,2,1,0:T(8,128)(2,1)S(1)}, u32[]{:S(2)}, u32[]{:S(2)}) %collective-permute-start) | collective-permute-done | bytes 196640 | tf_op jit(solution)/shard_map/while/body/eval_jaxpr/ppermute | solution.py:16
  238.4 6.0 %collective-permute-start.1 = (bf16[1,8,16,768]{3,2,1,0:T(8,128)(2,1)S(1)}, bf16[1,8,16,768]{3,2,1,0:T(8,128)(2,1)S(1)}, u32[]{:S(2)}, u32[]{:S(2)}) collective-permute-start(bf16[1,8,16,768]{3,2,1,0:T(8,128)(2,1)S(1)} %get-tuple-element.1098), channel_id=1, source_target_pairs={{8,0},{16,8},{24,16},{9,1},{17,9},{25,17},{10,2},{18,10},{26,18},{... | collective-permute-start | bytes 589832 | tf_op jit(solution)/shard_map/while/body/eval_jaxpr/ppermute | solution.py:16
  244.4 10.2 %conditional.4 = (bf16[1,8,16,768]{3,2,1,0:T(8,128)(2,1)S(1)}) conditional(s32[]{:T(128)} %convert_element_type.175, () %tuple.158, (pred[]{:T(512)}, bf16[4,1,8,16,768]{4,3,2,1,0:T(8,128)(2,1)S(1)}, s32[]{:T(128)}, bf16[1,8,16,768]{3,2,1,0:T(8,128)(2,1)S(1)}, s32[4]{0:T(128)S(1)}, /*index=5*/bf16[768]{0:T(1024)(128)(2,1)S(1)}, ...), branch_computations={%region_1.1_spmd, %region_2.4_spmd} | conditional | flops 617591168 | bytes 9590903 | solution.py:72
  250.9 3.7 %fusion.9 = f32[128,768]{1,0:T(8,128)S(1)} fusion(bf16[1536,768]{1,0:T(8,128)(2,1)} %get-tuple-element.678, f32[1536]{0:T(1024)S(1)} %fusion.114, bf16[128,768]{1,0:T(8,128)(2,1)S(1)} %bitcast.52, bf16[1536,768]{1,0:T(8,128)(2,1)} %get-tuple-element.677), kind=kOutput, calls=%fused_computation.58 | convolution fusion | flops 605945856 | bytes 5314560 | tf_op jit(solution)/shard_map/while/body/eval_jaxpr/cond/branch_1_fun/dot_general | solution.py:58
  256.1 6.1 %collective-permute-done = bf16[1,8,16,768]{3,2,1,0:T(8,128)(2,1)S(1)} collective-permute-done((bf16[1,8,16,768]{3,2,1,0:T(8,128)(2,1)S(1)}, bf16[1,8,16,768]{3,2,1,0:T(8,128)(2,1)S(1)}, u32[]{:S(2)}, u32[]{:S(2)}) %collective-permute-start) | collective-permute-done | bytes 196640 | tf_op jit(solution)/shard_map/while/body/eval_jaxpr/ppermute | solution.py:16
  (172 shorter events, 59.9 us)
Async XLA Ops:
  6.5 50.7 %all-gather.5.cloned.1.call-start = ((), (), s32[]{:S(2)}) async-start(), calls=%async_computation | async-start | bytes 2654208 | tf_op jit(solution)/shard_map/all_gather | solution.py:101
  7.3 66.7 %all-gather.7.cloned.1.call-start = ((), (), s32[]{:S(2)}) async-start(), calls=%async_computation.1 | async-start | bytes 2654208 | tf_op jit(solution)/shard_map/all_gather | solution.py:102
  8.0 98.4 %all-gather.9.cloned.1.call-start = ((), (), s32[]{:S(2)}) async-start(), calls=%async_computation.2 | async-start | bytes 2654208 | tf_op jit(solution)/shard_map/all_gather | solution.py:103
  8.1 9.0 %collective-permute-start.12 = (bf16[1,192,768]{2,1,0:T(8,128)(2,1)}, bf16[1,192,768]{2,1,0:T(8,128)(2,1)S(1)}, u32[]{:S(2)}, u32[]{:S(2)}) collective-permute-start(bf16[1,192,768]{2,1,0:T(8,128)(2,1)} %param.21), channel_id=1, source_target_pairs={{0,8},{8,0},{16,24},{24,16},{1,9},{9,1},{17,25},{25,17},{2,10},{10... | collective-permute-start | bytes 884744 | tf_op jit(solution)/shard_map/ppermute | solution.py:10
  17.1 7.9 %collective-permute-start.13 = (bf16[1,192,768]{2,1,0:T(8,128)(2,1)S(1)}, bf16[1,192,768]{2,1,0:T(8,128)(2,1)S(1)}, u32[]{:S(2)}, u32[]{:S(2)}) collective-permute-start(bf16[1,192,768]{2,1,0:T(8,128)(2,1)S(1)} %collective-permute-done.12), channel_id=1, source_target_pairs={{0,16},{8,24},{16,0},{24,8},{1,17},{9,25},{17,1},{25,9},{2,18},{10... | collective-permute-start | bytes 884744 | tf_op jit(solution)/shard_map/ppermute | solution.py:10
  25.7 112.9 %all-gather.11.cloned.1.call-start = ((), (), s32[]{:S(2)}) async-start(), calls=%async_computation.3 | async-start | bytes 2654208 | tf_op jit(solution)/shard_map/all_gather | solution.py:104
  25.8 7.4 %collective-permute-start.14 = (bf16[1,192,768]{2,1,0:T(8,128)(2,1)}, bf16[1,192,768]{2,1,0:T(8,128)(2,1)S(1)}, u32[]{:S(2)}, u32[]{:S(2)}) collective-permute-start(bf16[1,192,768]{2,1,0:T(8,128)(2,1)} %param.22), channel_id=1, source_target_pairs={{0,8},{8,0},{16,24},{24,16},{1,9},{9,1},{17,25},{25,17},{2,10},{10... | collective-permute-start | bytes 884744 | tf_op jit(solution)/shard_map/ppermute | solution.py:10
  33.2 6.7 %collective-permute-start.15 = (bf16[1,192,768]{2,1,0:T(8,128)(2,1)S(1)}, bf16[1,192,768]{2,1,0:T(8,128)(2,1)S(1)}, u32[]{:S(2)}, u32[]{:S(2)}) collective-permute-start(bf16[1,192,768]{2,1,0:T(8,128)(2,1)S(1)} %collective-permute-done.14), channel_id=1, source_target_pairs={{0,16},{8,24},{16,0},{24,8},{1,17},{9,25},{17,1},{25,9},{2,18},{10... | collective-permute-start | bytes 884744 | tf_op jit(solution)/shard_map/ppermute | solution.py:10
  40.6 4.8 %collective-permute-start.4 = (bf16[1,7,7,768]{3,2,1,0:T(8,128)(2,1)}, bf16[1,7,7,768]{3,2,1,0:T(8,128)(2,1)S(1)}, u32[]{:S(2)}, u32[]{:S(2)}) collective-permute-start(bf16[1,7,7,768]{3,2,1,0:T(8,128)(2,1)} %param.17), channel_id=1, source_target_pairs={{0,8},{8,0},{16,24},{24,16},{1,9},{9,1},{17,25},{25,17},{2,10},{10... | collective-permute-start | bytes 225800 | tf_op jit(solution)/shard_map/ppermute | solution.py:10
  45.4 11.7 %collective-permute-start.5 = (bf16[1,7,7,768]{3,2,1,0:T(8,128)(2,1)S(1)}, bf16[1,7,7,768]{3,2,1,0:T(8,128)(2,1)S(1)}, u32[]{:S(2)}, u32[]{:S(2)}) collective-permute-start(bf16[1,7,7,768]{3,2,1,0:T(8,128)(2,1)S(1)} %collective-permute-done.4), channel_id=1, source_target_pairs={{0,16},{8,24},{16,0},{24,8},{1,17},{9,25},{17,1},{25,9},{2,18},{10... | collective-permute-start | bytes 225800 | tf_op jit(solution)/shard_map/ppermute | solution.py:10
  48.8 4.7 %collective-permute-start.10 = (bf16[1,768]{1,0:T(2,128)(2,1)}, bf16[1,768]{1,0:T(2,128)(2,1)S(1)}, u32[]{:S(2)}, u32[]{:S(2)}) collective-permute-start(bf16[1,768]{1,0:T(2,128)(2,1)} %param.20), channel_id=1, source_target_pairs={{0,8},{8,0},{16,24},{24,16},{1,9},{9,1},{17,25},{25,17},{2,10},{10... | collective-permute-start | bytes 4616 | tf_op jit(solution)/shard_map/ppermute | solution.py:10
  50.0 6.9 %collective-permute-start.3 = (bf16[1,768]{1,0:T(2,128)(2,1)S(1)}, bf16[1,768]{1,0:T(2,128)(2,1)S(1)}, u32[]{:S(2)}, u32[]{:S(2)}) collective-permute-start(bf16[1,768]{1,0:T(2,128)(2,1)S(1)} %collective-permute-done.2), channel_id=1, source_target_pairs={{0,16},{8,24},{16,0},{24,8},{1,17},{9,25},{17,1},{25,9},{2,18},{10... | collective-permute-start | bytes 4616 | tf_op jit(solution)/shard_map/ppermute | solution.py:10
  51.5 5.4 %collective-permute-start.7 = (bf16[1,768]{1,0:T(2,128)(2,1)S(1)}, bf16[1,768]{1,0:T(2,128)(2,1)S(1)}, u32[]{:S(2)}, u32[]{:S(2)}) collective-permute-start(bf16[1,768]{1,0:T(2,128)(2,1)S(1)} %collective-permute-done.6), channel_id=1, source_target_pairs={{0,16},{8,24},{16,0},{24,8},{1,17},{9,25},{17,1},{25,9},{2,18},{10... | collective-permute-start | bytes 4616 | tf_op jit(solution)/shard_map/ppermute | solution.py:10
  52.1 4.9 %collective-permute-start.9 = (bf16[1,768]{1,0:T(2,128)(2,1)S(1)}, bf16[1,768]{1,0:T(2,128)(2,1)S(1)}, u32[]{:S(2)}, u32[]{:S(2)}) collective-permute-start(bf16[1,768]{1,0:T(2,128)(2,1)S(1)} %collective-permute-done.8), channel_id=1, source_target_pairs={{0,16},{8,24},{16,0},{24,8},{1,17},{9,25},{17,1},{25,9},{2,18},{10... | collective-permute-start | bytes 4616 | tf_op jit(solution)/shard_map/ppermute | solution.py:10
  149.0 6.1 %collective-permute-start.1 = (bf16[1,8,16,768]{3,2,1,0:T(8,128)(2,1)S(1)}, bf16[1,8,16,768]{3,2,1,0:T(8,128)(2,1)S(1)}, u32[]{:S(2)}, u32[]{:S(2)}) collective-permute-start(bf16[1,8,16,768]{3,2,1,0:T(8,128)(2,1)S(1)} %get-tuple-element.1098), channel_id=1, source_target_pairs={{8,0},{16,8},{24,16},{9,1},{17,9},{25,17},{10,2},{18,10},{26,18},{... | collective-permute-start | bytes 589832 | tf_op jit(solution)/shard_map/while/body/eval_jaxpr/ppermute | solution.py:16
  150.4 8.9 %collective-permute-start = (bf16[1,8,16,768]{3,2,1,0:T(8,128)(2,1)S(1)}, bf16[1,8,16,768]{3,2,1,0:T(8,128)(2,1)S(1)}, u32[]{:S(2)}, u32[]{:S(2)}) collective-permute-start(bf16[1,8,16,768]{3,2,1,0:T(8,128)(2,1)S(1)} %get-tuple-element.1097), channel_id=1, source_target_pairs={{0,8},{8,16},{16,24},{1,9},{9,17},{17,25},{2,10},{10,18},{18,26},{... | collective-permute-start | bytes 589832 | tf_op jit(solution)/shard_map/while/body/eval_jaxpr/ppermute | solution.py:16
  169.6 5.3 %collective-permute-start.1 = (bf16[1,8,16,768]{3,2,1,0:T(8,128)(2,1)S(1)}, bf16[1,8,16,768]{3,2,1,0:T(8,128)(2,1)S(1)}, u32[]{:S(2)}, u32[]{:S(2)}) collective-permute-start(bf16[1,8,16,768]{3,2,1,0:T(8,128)(2,1)S(1)} %get-tuple-element.1098), channel_id=1, source_target_pairs={{8,0},{16,8},{24,16},{9,1},{17,9},{25,17},{10,2},{18,10},{26,18},{... | collective-permute-start | bytes 589832 | tf_op jit(solution)/shard_map/while/body/eval_jaxpr/ppermute | solution.py:16
  171.1 8.6 %collective-permute-start = (bf16[1,8,16,768]{3,2,1,0:T(8,128)(2,1)S(1)}, bf16[1,8,16,768]{3,2,1,0:T(8,128)(2,1)S(1)}, u32[]{:S(2)}, u32[]{:S(2)}) collective-permute-start(bf16[1,8,16,768]{3,2,1,0:T(8,128)(2,1)S(1)} %get-tuple-element.1097), channel_id=1, source_target_pairs={{0,8},{8,16},{16,24},{1,9},{9,17},{17,25},{2,10},{10,18},{18,26},{... | collective-permute-start | bytes 589832 | tf_op jit(solution)/shard_map/while/body/eval_jaxpr/ppermute | solution.py:16
  179.7 15.7 %collective-permute-start.1 = (bf16[1,8,16,768]{3,2,1,0:T(8,128)(2,1)S(1)}, bf16[1,8,16,768]{3,2,1,0:T(8,128)(2,1)S(1)}, u32[]{:S(2)}, u32[]{:S(2)}) collective-permute-start(bf16[1,8,16,768]{3,2,1,0:T(8,128)(2,1)S(1)} %get-tuple-element.1098), channel_id=1, source_target_pairs={{8,0},{16,8},{24,16},{9,1},{17,9},{25,17},{10,2},{18,10},{26,18},{... | collective-permute-start | bytes 589832 | tf_op jit(solution)/shard_map/while/body/eval_jaxpr/ppermute | solution.py:16
  192.3 15.7 %collective-permute-start = (bf16[1,8,16,768]{3,2,1,0:T(8,128)(2,1)S(1)}, bf16[1,8,16,768]{3,2,1,0:T(8,128)(2,1)S(1)}, u32[]{:S(2)}, u32[]{:S(2)}) collective-permute-start(bf16[1,8,16,768]{3,2,1,0:T(8,128)(2,1)S(1)} %get-tuple-element.1097), channel_id=1, source_target_pairs={{0,8},{8,16},{16,24},{1,9},{9,17},{17,25},{2,10},{10,18},{18,26},{... | collective-permute-start | bytes 589832 | tf_op jit(solution)/shard_map/while/body/eval_jaxpr/ppermute | solution.py:16
  208.0 16.5 %collective-permute-start.1 = (bf16[1,8,16,768]{3,2,1,0:T(8,128)(2,1)S(1)}, bf16[1,8,16,768]{3,2,1,0:T(8,128)(2,1)S(1)}, u32[]{:S(2)}, u32[]{:S(2)}) collective-permute-start(bf16[1,8,16,768]{3,2,1,0:T(8,128)(2,1)S(1)} %get-tuple-element.1098), channel_id=1, source_target_pairs={{8,0},{16,8},{24,16},{9,1},{17,9},{25,17},{10,2},{18,10},{26,18},{... | collective-permute-start | bytes 589832 | tf_op jit(solution)/shard_map/while/body/eval_jaxpr/ppermute | solution.py:16
  223.1 15.3 %collective-permute-start = (bf16[1,8,16,768]{3,2,1,0:T(8,128)(2,1)S(1)}, bf16[1,8,16,768]{3,2,1,0:T(8,128)(2,1)S(1)}, u32[]{:S(2)}, u32[]{:S(2)}) collective-permute-start(bf16[1,8,16,768]{3,2,1,0:T(8,128)(2,1)S(1)} %get-tuple-element.1097), channel_id=1, source_target_pairs={{0,8},{8,16},{16,24},{1,9},{9,17},{17,25},{2,10},{10,18},{18,26},{... | collective-permute-start | bytes 589832 | tf_op jit(solution)/shard_map/while/body/eval_jaxpr/ppermute | solution.py:16
  238.4 17.7 %collective-permute-start.1 = (bf16[1,8,16,768]{3,2,1,0:T(8,128)(2,1)S(1)}, bf16[1,8,16,768]{3,2,1,0:T(8,128)(2,1)S(1)}, u32[]{:S(2)}, u32[]{:S(2)}) collective-permute-start(bf16[1,8,16,768]{3,2,1,0:T(8,128)(2,1)S(1)} %get-tuple-element.1098), channel_id=1, source_target_pairs={{8,0},{16,8},{24,16},{9,1},{17,9},{25,17},{10,2},{18,10},{26,18},{... | collective-permute-start | bytes 589832 | tf_op jit(solution)/shard_map/while/body/eval_jaxpr/ppermute | solution.py:16
  254.6 7.6 %collective-permute-start = (bf16[1,8,16,768]{3,2,1,0:T(8,128)(2,1)S(1)}, bf16[1,8,16,768]{3,2,1,0:T(8,128)(2,1)S(1)}, u32[]{:S(2)}, u32[]{:S(2)}) collective-permute-start(bf16[1,8,16,768]{3,2,1,0:T(8,128)(2,1)S(1)} %get-tuple-element.1097), channel_id=1, source_target_pairs={{0,8},{8,16},{16,24},{1,9},{9,17},{17,25},{2,10},{10,18},{18,26},{... | collective-permute-start | bytes 589832 | tf_op jit(solution)/shard_map/while/body/eval_jaxpr/ppermute | solution.py:16
  (10 other events, 415.3 us)
Sparse Core Ops, SparseCore 0:
  9.0 32.6 all-gather.4
  43.3 30.6 all-gather.6
  75.6 30.6 all-gather.8
  107.9 30.6 all-gather.10
where the time goes:
time: 270 us
  waiting for transfers between devices  165 us (61%)
  starting transfers between devices  44.2 us (16%)
  other arithmetic  19.5 us (7%)
  matrix products  14.7 us (5%)
  between operations  13.2 us (5%)
  local copies, waits for them, and re-layouts  7.06 us (3%)
  loops' own time  6.28 us (2%)
    ppermute x10, waiting for transfers between devices, passed_along(): lax.ppermute(value, axis, [(source, source + steps) for source in range(i...  48.6 us
    ppermute x14, waiting for transfers between devices, swapped(): return lax.ppermute(value, axis, pairs)  33.2 us
    ppermute x10, starting transfers between devices, passed_along(): lax.ppermute(value, axis, [(source, source + steps) for source in range(i...  32.6 us
    all_gather x1, waiting for transfers between devices, on_device(): lax.all_gather(shards[0], 'dp', axis=1, tiled=True)  32.4 us
    all_gather x1, waiting for transfers between devices, on_device(): lax.all_gather(shards[1], 'dp', axis=1, tiled=True)  32.2 us
    all_gather x1, waiting for transfers between devices, on_device(): lax.all_gather(w_out, 'dp', axis=1, tiled=True)  16.8 us
    dot_general x4, matrix products, conv_block(): jnp.dot(activated, w_out, preferred_element_type=jnp.float32)  14.7 us
    reduce_sum x4, other arithmetic, conv_block(): average = jnp.sum(spatial, axis=-1, keepdims=True) / channel_count  13.8 us
  transfers between devices with their start and end apart: 28, of which 17 were waited for; matrix products, arithmetic and copies ran while one was open for 8% of the time, Pallas kernels for 0%

commit v1 on v0

--- a/solution.py
+++ b/solution.py
@@ -97,10 +97,24 @@
             "section",
             bit_index,
         )
+
+    def _produce_roots(work_x, peer_axis):
+        prior, piece_now = (lax.axis_size(peer_axis), lax.axis_index(peer_axis))
+        upper, work_now = (work_x, 1)
+        while work_now < prior:
+            taken_in = lax.ppermute(
+                upper, axis_name=peer_axis, perm=[(i, i ^ work_now) for i in range(prior)]
+            )
+            low = jnp.concatenate([upper, taken_in], 1)
+            arr_out = jnp.concatenate([taken_in, upper], 1)
+            upper = jnp.where(piece_now & work_now == 0, low, arr_out)
+            work_now = 2 * work_now
+        return upper
+
     full_in, full_out, mirror_in, mirror_out = (
         lax.all_gather(w_in, "dp", axis=1, tiled=True),
         lax.all_gather(w_out, "dp", axis=1, tiled=True),
-        lax.all_gather(shards[0], "dp", axis=1, tiled=True),
+        _produce_roots(shards[0], "dp"),
         lax.all_gather(shards[1], "dp", axis=1, tiled=True),
     )
     own_params = (

time: 270 us -> 279 us (1.033)
  starting transfers between devices: 44.2 us -> 52.8 us
    ppermute x0 -> x3, waiting for transfers between devices: none -> 82.6 us  [_produce_roots(): lax.ppermute(upper, axis_name=peer_axis, perm=[(i, i ^ work_now) for i in...]
    all_gather x1 -> x0, waiting for transfers between devices: 32.4 us -> none  [on_device(): lax.all_gather(shards[0], 'dp', axis=1, tiled=True)]
    all_gather x1, waiting for transfers between devices: 32.2 us -> 0.01 us  [on_device(): lax.all_gather(shards[1], 'dp', axis=1, tiled=True)]
    all_gather x1, waiting for transfers between devices: 16.8 us -> 0.01 us  [on_device(): lax.all_gather(w_out, 'dp', axis=1, tiled=True)]
    ppermute x0 -> x3, starting transfers between devices: none -> 7.37 us  [_produce_roots(): lax.ppermute(upper, axis_name=peer_axis, perm=[(i, i ^ work_now) for i in...]
    select_n x0 -> x5, other arithmetic: none -> 4.09 us  [_produce_roots(): upper = jnp.where(piece_now & work_now == 0, low, arr_out)]
  transfers between devices with their start and end apart: 28 -> 30, of which waited for: 17 -> 20; matrix products, arithmetic and copies ran while one was open for 8% -> 8% of each run, Pallas kernels for 0% -> 0%
where the time goes in v1:
time: 279 us; the launch traced here: 278 us
  waiting for transfers between devices  164 us (59%)
  starting transfers between devices  52.8 us (19%)
  other arithmetic  20.8 us (7%)
  matrix products  14.7 us (5%)
  between operations  13.2 us (5%)
  loops' own time  6.3 us (2%)
  local copies, waits for them, and re-layouts  6.26 us (2%)
    ppermute x3, waiting for transfers between devices, _produce_roots(): lax.ppermute(upper, axis_name=peer_axis, perm=[(i, i ^ work_now) for i in...  82.6 us
    ppermute x10, waiting for transfers between devices, passed_along(): lax.ppermute(value, axis, [(source, source + steps) for source in range(i...  47 us
    ppermute x10, starting transfers between devices, passed_along(): lax.ppermute(value, axis, [(source, source + steps) for source in range(i...  33.6 us
    ppermute x14, waiting for transfers between devices, swapped(): return lax.ppermute(value, axis, pairs)  33 us
    dot_general x4, matrix products, conv_block(): jnp.dot(activated, w_out, preferred_element_type=jnp.float32)  14.7 us
    reduce_sum x4, other arithmetic, conv_block(): average = jnp.sum(spatial, axis=-1, keepdims=True) / channel_count  13.8 us
    ppermute x14, starting transfers between devices, swapped(): return lax.ppermute(value, axis, pairs)  11.7 us
    ppermute x3, starting transfers between devices, _produce_roots(): lax.ppermute(upper, axis_name=peer_axis, perm=[(i, i ^ work_now) for i in...  7.37 us
  transfers between devices with their start and end apart: 30, of which 20 were waited for; matrix products, arithmetic and copies ran while one was open for 8% of the time, Pallas kernels for 0%

profile of v1, /device:TPU:6, one launch (start us, length us, event | category | flops | bytes accessed | tf_op | source)
XLA Modules:
  0.0 278.1 jit_solution(16417299209188390887)
XLA Ops:
  8.7 8.4 %collective-permute-done.17 = bf16[1,192,768]{2,1,0:T(8,128)(2,1)S(1)} collective-permute-done((bf16[1,192,768]{2,1,0:T(8,128)(2,1)}, bf16[1,192,768]{2,1,0:T(8,128)(2,1)S(1)}, u32[]{:S(2)}, u32[]{:S(2)}) %collective-permute-start.17) | collective-permute-done | bytes 294944 | tf_op jit(solution)/shard_map/ppermute | solution.py:10
  17.6 7.4 %collective-permute-done.18 = bf16[1,192,768]{2,1,0:T(8,128)(2,1)S(1)} collective-permute-done((bf16[1,192,768]{2,1,0:T(8,128)(2,1)S(1)}, bf16[1,192,768]{2,1,0:T(8,128)(2,1)S(1)}, u32[]{:S(2)}, u32[]{:S(2)}) %collective-permute-start.18) | collective-permute-done | bytes 294944 | tf_op jit(solution)/shard_map/ppermute | solution.py:10
  26.3 6.8 %collective-permute-done.12 = bf16[1,192,768]{2,1,0:T(8,128)(2,1)S(1)} collective-permute-done((bf16[1,192,768]{2,1,0:T(8,128)(2,1)}, bf16[1,192,768]{2,1,0:T(8,128)(2,1)S(1)}, u32[]{:S(2)}, u32[]{:S(2)}) %collective-permute-start.12) | collective-permute-done | bytes 294944 | tf_op jit(solution)/shard_map/ppermute | solution.py:10
  33.6 6.2 %collective-permute-done.13 = bf16[1,192,768]{2,1,0:T(8,128)(2,1)S(1)} collective-permute-done((bf16[1,192,768]{2,1,0:T(8,128)(2,1)S(1)}, bf16[1,192,768]{2,1,0:T(8,128)(2,1)S(1)}, u32[]{:S(2)}, u32[]{:S(2)}) %collective-permute-start.13) | collective-permute-done | bytes 294944 | tf_op jit(solution)/shard_map/ppermute | solution.py:10
  43.4 24.3 %collective-permute-done.15 = bf16[1,384,768]{2,1,0:T(8,128)(2,1)S(1)} collective-permute-done((bf16[1,384,768]{2,1,0:T(8,128)(2,1)S(1)}, bf16[1,384,768]{2,1,0:T(8,128)(2,1)S(1)}, u32[]{:S(2)}, u32[]{:S(2)}) %collective-permute-start.15) | collective-permute-done | bytes 589856 | tf_op jit(solution)/shard_map/ppermute | solution.py:105
  69.2 5.7 %collective-permute-start.16 = (bf16[1,768,768]{2,1,0:T(8,128)(2,1)}, bf16[1,768,768]{2,1,0:T(8,128)(2,1)S(1)}, u32[]{:S(2)}, u32[]{:S(2)}) collective-permute-start(bf16[1,768,768]{2,1,0:T(8,128)(2,1)} %maximum_select_fusion.2), channel_id=1, source_target_pairs={{0,4},{1,5},{2,6},{3,7},{4,0},{5,1},{6,2},{7,3},{8,12},{9,13},{10,... | collective-permute-start | bytes 3538952 | tf_op jit(solution)/shard_map/ppermute | solution.py:105
  89.2 56.8 %collective-permute-done.16 = bf16[1,768,768]{2,1,0:T(8,128)(2,1)S(1)} collective-permute-done((bf16[1,768,768]{2,1,0:T(8,128)(2,1)}, bf16[1,768,768]{2,1,0:T(8,128)(2,1)S(1)}, u32[]{:S(2)}, u32[]{:S(2)}) %collective-permute-start.16) | collective-permute-done | bytes 1179680 | tf_op jit(solution)/shard_map/ppermute | solution.py:105
  148.0 122.7 %while.19 = (s32[]{:T(128)}, bf16[1,8,16,768]{3,2,1,0:T(8,128)(2,1)S(1)}, bf16[1,8,16,768]{3,2,1,0:T(8,128)(2,1)S(1)}, bf16[4,1,8,16,768]{4,3,2,1,0:T(8,128)(2,1...) while((s32[]{:T(128)}, ...), condition=%wide.region_9.10_spmd, body=%wide.region_0.9_spmd.sunk | while | flops 1235378944 | bytes 22721452 | solution.py:170
  148.0 10.1 %conditional.5 = (bf16[1,8,16,768]{3,2,1,0:T(8,128)(2,1)S(1)}) conditional(s32[]{:T(128)} %convert_element_type.176, () %tuple.160, (pred[]{:T(512)}, bf16[4,1,8,16,768]{4,3,2,1,0:T(8,128)(2,1)S(1)}, s32[]{:T(128)}, bf16[1,8,16,768]{3,2,1,0:T(8,128)(2,1)S(1)}, s32[4]{0:T(128)S(1)}, /*index=5*/bf16[768]{0:T(1024)(128)(2,1)S(1)}, ...), branch_computations={%region_5.5_spmd, %region_6.8_spmd} | conditional | flops 617591168 | bytes 9590903 | solution.py:72
  154.4 3.7 %fusion.129 = f32[128,768]{1,0:T(8,128)S(1)} fusion(bf16[1536,768]{1,0:T(8,128)(2,1)} %get-tuple-element.690, f32[1536]{0:T(1024)S(1)} %fusion.234, bf16[128,768]{1,0:T(8,128)(2,1)S(1)} %bitcast.56, bf16[1536,768]{1,0:T(8,128)(2,1)} %get-tuple-element.689), kind=kOutput, calls=%fused_computation.285 | convolution fusion | flops 605945856 | bytes 5314560 | tf_op jit(solution)/shard_map/while/body/eval_jaxpr/cond/branch_1_fun/dot_general | solution.py:58
  163.3 4.2 %collective-permute-done = bf16[1,8,16,768]{3,2,1,0:T(8,128)(2,1)S(1)} collective-permute-done((bf16[1,8,16,768]{3,2,1,0:T(8,128)(2,1)S(1)}, bf16[1,8,16,768]{3,2,1,0:T(8,128)(2,1)S(1)}, u32[]{:S(2)}, u32[]{:S(2)}) %collective-permute-start) | collective-permute-done | bytes 196640 | tf_op jit(solution)/shard_map/while/body/eval_jaxpr/ppermute | solution.py:16
  167.5 10.1 %conditional.5 = (bf16[1,8,16,768]{3,2,1,0:T(8,128)(2,1)S(1)}) conditional(s32[]{:T(128)} %convert_element_type.176, () %tuple.160, (pred[]{:T(512)}, bf16[4,1,8,16,768]{4,3,2,1,0:T(8,128)(2,1)S(1)}, s32[]{:T(128)}, bf16[1,8,16,768]{3,2,1,0:T(8,128)(2,1)S(1)}, s32[4]{0:T(128)S(1)}, /*index=5*/bf16[768]{0:T(1024)(128)(2,1)S(1)}, ...), branch_computations={%region_5.5_spmd, %region_6.8_spmd} | conditional | flops 617591168 | bytes 9590903 | solution.py:72
  173.8 3.7 %fusion.129 = f32[128,768]{1,0:T(8,128)S(1)} fusion(bf16[1536,768]{1,0:T(8,128)(2,1)} %get-tuple-element.690, f32[1536]{0:T(1024)S(1)} %fusion.234, bf16[128,768]{1,0:T(8,128)(2,1)S(1)} %bitcast.56, bf16[1536,768]{1,0:T(8,128)(2,1)} %get-tuple-element.689), kind=kOutput, calls=%fused_computation.285 | convolution fusion | flops 605945856 | bytes 5314560 | tf_op jit(solution)/shard_map/while/body/eval_jaxpr/cond/branch_1_fun/dot_general | solution.py:58
  182.2 4.7 %collective-permute-done = bf16[1,8,16,768]{3,2,1,0:T(8,128)(2,1)S(1)} collective-permute-done((bf16[1,8,16,768]{3,2,1,0:T(8,128)(2,1)S(1)}, bf16[1,8,16,768]{3,2,1,0:T(8,128)(2,1)S(1)}, u32[]{:S(2)}, u32[]{:S(2)}) %collective-permute-start) | collective-permute-done | bytes 196640 | tf_op jit(solution)/shard_map/while/body/eval_jaxpr/ppermute | solution.py:16
  186.9 12.7 %collective-permute-start.1 = (bf16[1,8,16,768]{3,2,1,0:T(8,128)(2,1)S(1)}, bf16[1,8,16,768]{3,2,1,0:T(8,128)(2,1)S(1)}, u32[]{:S(2)}, u32[]{:S(2)}) collective-permute-start(bf16[1,8,16,768]{3,2,1,0:T(8,128)(2,1)S(1)} %get-tuple-element.1098), channel_id=1, source_target_pairs={{8,0},{16,8},{24,16},{9,1},{17,9},{25,17},{10,2},{18,10},{26,18},{... | collective-permute-start | bytes 589832 | tf_op jit(solution)/shard_map/while/body/eval_jaxpr/ppermute | solution.py:16
  202.7 12.8 %collective-permute-done = bf16[1,8,16,768]{3,2,1,0:T(8,128)(2,1)S(1)} collective-permute-done((bf16[1,8,16,768]{3,2,1,0:T(8,128)(2,1)S(1)}, bf16[1,8,16,768]{3,2,1,0:T(8,128)(2,1)S(1)}, u32[]{:S(2)}, u32[]{:S(2)}) %collective-permute-start) | collective-permute-done | bytes 196640 | tf_op jit(solution)/shard_map/while/body/eval_jaxpr/ppermute | solution.py:16
  215.6 4.8 %collective-permute-start.1 = (bf16[1,8,16,768]{3,2,1,0:T(8,128)(2,1)S(1)}, bf16[1,8,16,768]{3,2,1,0:T(8,128)(2,1)S(1)}, u32[]{:S(2)}, u32[]{:S(2)}) collective-permute-start(bf16[1,8,16,768]{3,2,1,0:T(8,128)(2,1)S(1)} %get-tuple-element.1098), channel_id=1, source_target_pairs={{8,0},{16,8},{24,16},{9,1},{17,9},{25,17},{10,2},{18,10},{26,18},{... | collective-permute-start | bytes 589832 | tf_op jit(solution)/shard_map/while/body/eval_jaxpr/ppermute | solution.py:16
  220.4 10.3 %conditional.4 = (bf16[1,8,16,768]{3,2,1,0:T(8,128)(2,1)S(1)}) conditional(s32[]{:T(128)} %convert_element_type.175, () %tuple.158, (pred[]{:T(512)}, bf16[4,1,8,16,768]{4,3,2,1,0:T(8,128)(2,1)S(1)}, s32[]{:T(128)}, bf16[1,8,16,768]{3,2,1,0:T(8,128)(2,1)S(1)}, s32[4]{0:T(128)S(1)}, /*index=5*/bf16[768]{0:T(1024)(128)(2,1)S(1)}, ...), branch_computations={%region_1.1_spmd, %region_2.4_spmd} | conditional | flops 617591168 | bytes 9590903 | solution.py:72
  226.9 3.7 %fusion.9 = f32[128,768]{1,0:T(8,128)S(1)} fusion(bf16[1536,768]{1,0:T(8,128)(2,1)} %get-tuple-element.678, f32[1536]{0:T(1024)S(1)} %fusion.114, bf16[128,768]{1,0:T(8,128)(2,1)S(1)} %bitcast.57, bf16[1536,768]{1,0:T(8,128)(2,1)} %get-tuple-element.677), kind=kOutput, calls=%fused_computation.58 | convolution fusion | flops 605945856 | bytes 5314560 | tf_op jit(solution)/shard_map/while/body/eval_jaxpr/cond/branch_1_fun/dot_general | solution.py:58
  232.2 13.7 %collective-permute-done = bf16[1,8,16,768]{3,2,1,0:T(8,128)(2,1)S(1)} collective-permute-done((bf16[1,8,16,768]{3,2,1,0:T(8,128)(2,1)S(1)}, bf16[1,8,16,768]{3,2,1,0:T(8,128)(2,1)S(1)}, u32[]{:S(2)}, u32[]{:S(2)}) %collective-permute-start) | collective-permute-done | bytes 196640 | tf_op jit(solution)/shard_map/while/body/eval_jaxpr/ppermute | solution.py:16
  245.9 6.9 %collective-permute-start.1 = (bf16[1,8,16,768]{3,2,1,0:T(8,128)(2,1)S(1)}, bf16[1,8,16,768]{3,2,1,0:T(8,128)(2,1)S(1)}, u32[]{:S(2)}, u32[]{:S(2)}) collective-permute-start(bf16[1,8,16,768]{3,2,1,0:T(8,128)(2,1)S(1)} %get-tuple-element.1098), channel_id=1, source_target_pairs={{8,0},{16,8},{24,16},{9,1},{17,9},{25,17},{10,2},{18,10},{26,18},{... | collective-permute-start | bytes 589832 | tf_op jit(solution)/shard_map/while/body/eval_jaxpr/ppermute | solution.py:16
  252.8 10.3 %conditional.4 = (bf16[1,8,16,768]{3,2,1,0:T(8,128)(2,1)S(1)}) conditional(s32[]{:T(128)} %convert_element_type.175, () %tuple.158, (pred[]{:T(512)}, bf16[4,1,8,16,768]{4,3,2,1,0:T(8,128)(2,1)S(1)}, s32[]{:T(128)}, bf16[1,8,16,768]{3,2,1,0:T(8,128)(2,1)S(1)}, s32[4]{0:T(128)S(1)}, /*index=5*/bf16[768]{0:T(1024)(128)(2,1)S(1)}, ...), branch_computations={%region_1.1_spmd, %region_2.4_spmd} | conditional | flops 617591168 | bytes 9590903 | solution.py:72
  259.4 3.7 %fusion.9 = f32[128,768]{1,0:T(8,128)S(1)} fusion(bf16[1536,768]{1,0:T(8,128)(2,1)} %get-tuple-element.678, f32[1536]{0:T(1024)S(1)} %fusion.114, bf16[128,768]{1,0:T(8,128)(2,1)S(1)} %bitcast.57, bf16[1536,768]{1,0:T(8,128)(2,1)} %get-tuple-element.677), kind=kOutput, calls=%fused_computation.58 | convolution fusion | flops 605945856 | bytes 5314560 | tf_op jit(solution)/shard_map/while/body/eval_jaxpr/cond/branch_1_fun/dot_general | solution.py:58
  264.6 6.1 %collective-permute-done = bf16[1,8,16,768]{3,2,1,0:T(8,128)(2,1)S(1)} collective-permute-done((bf16[1,8,16,768]{3,2,1,0:T(8,128)(2,1)S(1)}, bf16[1,8,16,768]{3,2,1,0:T(8,128)(2,1)S(1)}, u32[]{:S(2)}, u32[]{:S(2)}) %collective-permute-start) | collective-permute-done | bytes 196640 | tf_op jit(solution)/shard_map/while/body/eval_jaxpr/ppermute | solution.py:16
  (186 shorter events, 62.5 us)
Async XLA Ops:
  6.5 141.3 %all-gather.4.cloned.1.call-start = ((), (), s32[]{:S(2)}) async-start(), calls=%async_computation | async-start | bytes 2654208 | tf_op jit(solution)/shard_map/all_gather | solution.py:115
  7.3 140.6 %all-gather.6.cloned.1.call-start = ((), (), s32[]{:S(2)}) async-start(), calls=%async_computation.1 | async-start | bytes 2654208 | tf_op jit(solution)/shard_map/all_gather | solution.py:116
  8.0 139.8 %all-gather.8.cloned.1.call-start = ((), (), s32[]{:S(2)}) async-start(), calls=%async_computation.2 | async-start | bytes 2654208 | tf_op jit(solution)/shard_map/all_gather | solution.py:118
  8.1 9.0 %collective-permute-start.17 = (bf16[1,192,768]{2,1,0:T(8,128)(2,1)}, bf16[1,192,768]{2,1,0:T(8,128)(2,1)S(1)}, u32[]{:S(2)}, u32[]{:S(2)}) collective-permute-start(bf16[1,192,768]{2,1,0:T(8,128)(2,1)} %param.22), channel_id=1, source_target_pairs={{0,8},{8,0},{16,24},{24,16},{1,9},{9,1},{17,25},{25,17},{2,10},{10... | collective-permute-start | bytes 884744 | tf_op jit(solution)/shard_map/ppermute | solution.py:10
  17.1 7.9 %collective-permute-start.18 = (bf16[1,192,768]{2,1,0:T(8,128)(2,1)S(1)}, bf16[1,192,768]{2,1,0:T(8,128)(2,1)S(1)}, u32[]{:S(2)}, u32[]{:S(2)}) collective-permute-start(bf16[1,192,768]{2,1,0:T(8,128)(2,1)S(1)} %collective-permute-done.17), channel_id=1, source_target_pairs={{0,16},{8,24},{16,0},{24,8},{1,17},{9,25},{17,1},{25,9},{2,18},{10... | collective-permute-start | bytes 884744 | tf_op jit(solution)/shard_map/ppermute | solution.py:10
  25.7 7.4 %collective-permute-start.12 = (bf16[1,192,768]{2,1,0:T(8,128)(2,1)}, bf16[1,192,768]{2,1,0:T(8,128)(2,1)S(1)}, u32[]{:S(2)}, u32[]{:S(2)}) collective-permute-start(bf16[1,192,768]{2,1,0:T(8,128)(2,1)} %param.21), channel_id=1, source_target_pairs={{0,8},{8,0},{16,24},{24,16},{1,9},{9,1},{17,25},{25,17},{2,10},{10... | collective-permute-start | bytes 884744 | tf_op jit(solution)/shard_map/ppermute | solution.py:10
  33.1 6.7 %collective-permute-start.13 = (bf16[1,192,768]{2,1,0:T(8,128)(2,1)S(1)}, bf16[1,192,768]{2,1,0:T(8,128)(2,1)S(1)}, u32[]{:S(2)}, u32[]{:S(2)}) collective-permute-start(bf16[1,192,768]{2,1,0:T(8,128)(2,1)S(1)} %collective-permute-done.12), channel_id=1, source_target_pairs={{0,16},{8,24},{16,0},{24,8},{1,17},{9,25},{17,1},{25,9},{2,18},{10... | collective-permute-start | bytes 884744 | tf_op jit(solution)/shard_map/ppermute | solution.py:10
  41.6 26.1 %collective-permute-start.15 = (bf16[1,384,768]{2,1,0:T(8,128)(2,1)S(1)}, bf16[1,384,768]{2,1,0:T(8,128)(2,1)S(1)}, u32[]{:S(2)}, u32[]{:S(2)}) collective-permute-start(bf16[1,384,768]{2,1,0:T(8,128)(2,1)S(1)} %maximum_select_fusion.4), channel_id=1, source_target_pairs={{0,2},{1,3},{2,0},{3,1},{4,6},{5,7},{6,4},{7,5},{8,10},{9,11},{10,... | collective-permute-start | bytes 1769480 | tf_op jit(solution)/shard_map/ppermute | solution.py:105
  69.2 76.8 %collective-permute-start.16 = (bf16[1,768,768]{2,1,0:T(8,128)(2,1)}, bf16[1,768,768]{2,1,0:T(8,128)(2,1)S(1)}, u32[]{:S(2)}, u32[]{:S(2)}) collective-permute-start(bf16[1,768,768]{2,1,0:T(8,128)(2,1)} %maximum_select_fusion.2), channel_id=1, source_target_pairs={{0,4},{1,5},{2,6},{3,7},{4,0},{5,1},{6,2},{7,3},{8,12},{9,13},{10,... | collective-permute-start | bytes 3538952 | tf_op jit(solution)/shard_map/ppermute | solution.py:105
  74.9 12.9 %collective-permute-start.4 = (bf16[1,7,7,768]{3,2,1,0:T(8,128)(2,1)S(1)}, bf16[1,7,7,768]{3,2,1,0:T(8,128)(2,1)S(1)}, u32[]{:S(2)}, u32[]{:S(2)}) collective-permute-start(bf16[1,7,7,768]{3,2,1,0:T(8,128)(2,1)S(1)} %copy-done.2), channel_id=1, source_target_pairs={{0,8},{8,0},{16,24},{24,16},{1,9},{9,1},{17,25},{25,17},{2,10},{10... | collective-permute-start | bytes 225800 | tf_op jit(solution)/shard_map/ppermute | solution.py:10
  75.4 4.0 %collective-permute-start.2 = (bf16[1,768]{1,0:T(2,128)(2,1)S(1)}, bf16[1,768]{1,0:T(2,128)(2,1)S(1)}, u32[]{:S(2)}, u32[]{:S(2)}) collective-permute-start(bf16[1,768]{1,0:T(2,128)(2,1)S(1)} %copy-done.4), channel_id=1, source_target_pairs={{0,8},{8,0},{16,24},{24,16},{1,9},{9,1},{17,25},{25,17},{2,10},{10... | collective-permute-start | bytes 4616 | tf_op jit(solution)/shard_map/ppermute | solution.py:10
  77.0 3.6 %collective-permute-start.6 = (bf16[1,768]{1,0:T(2,128)(2,1)S(1)}, bf16[1,768]{1,0:T(2,128)(2,1)S(1)}, u32[]{:S(2)}, u32[]{:S(2)}) collective-permute-start(bf16[1,768]{1,0:T(2,128)(2,1)S(1)} %copy-done.5), channel_id=1, source_target_pairs={{0,8},{8,0},{16,24},{24,16},{1,9},{9,1},{17,25},{25,17},{2,10},{10... | collective-permute-start | bytes 4616 | tf_op jit(solution)/shard_map/ppermute | solution.py:10
  81.1 4.1 %collective-permute-start.7 = (bf16[1,768]{1,0:T(2,128)(2,1)S(1)}, bf16[1,768]{1,0:T(2,128)(2,1)S(1)}, u32[]{:S(2)}, u32[]{:S(2)}) collective-permute-start(bf16[1,768]{1,0:T(2,128)(2,1)S(1)} %collective-permute-done.6), channel_id=1, source_target_pairs={{0,16},{8,24},{16,0},{24,8},{1,17},{9,25},{17,1},{25,9},{2,18},{10... | collective-permute-start | bytes 4616 | tf_op jit(solution)/shard_map/ppermute | solution.py:10
  87.8 60.0 %collective-permute-start.5 = (bf16[1,7,7,768]{3,2,1,0:T(8,128)(2,1)S(1)}, bf16[1,7,7,768]{3,2,1,0:T(8,128)(2,1)S(1)}, u32[]{:S(2)}, u32[]{:S(2)}) collective-permute-start(bf16[1,7,7,768]{3,2,1,0:T(8,128)(2,1)S(1)} %collective-permute-done.4), channel_id=1, source_target_pairs={{0,16},{8,24},{16,0},{24,8},{1,17},{9,25},{17,1},{25,9},{2,18},{10... | collective-permute-start | bytes 225800 | tf_op jit(solution)/shard_map/ppermute | solution.py:10
  158.1 5.2 %collective-permute-start.1 = (bf16[1,8,16,768]{3,2,1,0:T(8,128)(2,1)S(1)}, bf16[1,8,16,768]{3,2,1,0:T(8,128)(2,1)S(1)}, u32[]{:S(2)}, u32[]{:S(2)}) collective-permute-start(bf16[1,8,16,768]{3,2,1,0:T(8,128)(2,1)S(1)} %get-tuple-element.1098), channel_id=1, source_target_pairs={{8,0},{16,8},{24,16},{9,1},{17,9},{25,17},{10,2},{18,10},{26,18},{... | collective-permute-start | bytes 589832 | tf_op jit(solution)/shard_map/while/body/eval_jaxpr/ppermute | solution.py:16
  159.5 8.0 %collective-permute-start = (bf16[1,8,16,768]{3,2,1,0:T(8,128)(2,1)S(1)}, bf16[1,8,16,768]{3,2,1,0:T(8,128)(2,1)S(1)}, u32[]{:S(2)}, u32[]{:S(2)}) collective-permute-start(bf16[1,8,16,768]{3,2,1,0:T(8,128)(2,1)S(1)} %get-tuple-element.1097), channel_id=1, source_target_pairs={{0,8},{8,16},{16,24},{1,9},{9,17},{17,25},{2,10},{10,18},{18,26},{... | collective-permute-start | bytes 589832 | tf_op jit(solution)/shard_map/while/body/eval_jaxpr/ppermute | solution.py:16
  177.5 4.6 %collective-permute-start.1 = (bf16[1,8,16,768]{3,2,1,0:T(8,128)(2,1)S(1)}, bf16[1,8,16,768]{3,2,1,0:T(8,128)(2,1)S(1)}, u32[]{:S(2)}, u32[]{:S(2)}) collective-permute-start(bf16[1,8,16,768]{3,2,1,0:T(8,128)(2,1)S(1)} %get-tuple-element.1098), channel_id=1, source_target_pairs={{8,0},{16,8},{24,16},{9,1},{17,9},{25,17},{10,2},{18,10},{26,18},{... | collective-permute-start | bytes 589832 | tf_op jit(solution)/shard_map/while/body/eval_jaxpr/ppermute | solution.py:16
  179.1 7.8 %collective-permute-start = (bf16[1,8,16,768]{3,2,1,0:T(8,128)(2,1)S(1)}, bf16[1,8,16,768]{3,2,1,0:T(8,128)(2,1)S(1)}, u32[]{:S(2)}, u32[]{:S(2)}) collective-permute-start(bf16[1,8,16,768]{3,2,1,0:T(8,128)(2,1)S(1)} %get-tuple-element.1097), channel_id=1, source_target_pairs={{0,8},{8,16},{16,24},{1,9},{9,17},{17,25},{2,10},{10,18},{18,26},{... | collective-permute-start | bytes 589832 | tf_op jit(solution)/shard_map/while/body/eval_jaxpr/ppermute | solution.py:16
  186.9 15.8 %collective-permute-start.1 = (bf16[1,8,16,768]{3,2,1,0:T(8,128)(2,1)S(1)}, bf16[1,8,16,768]{3,2,1,0:T(8,128)(2,1)S(1)}, u32[]{:S(2)}, u32[]{:S(2)}) collective-permute-start(bf16[1,8,16,768]{3,2,1,0:T(8,128)(2,1)S(1)} %get-tuple-element.1098), channel_id=1, source_target_pairs={{8,0},{16,8},{24,16},{9,1},{17,9},{25,17},{10,2},{18,10},{26,18},{... | collective-permute-start | bytes 589832 | tf_op jit(solution)/shard_map/while/body/eval_jaxpr/ppermute | solution.py:16
  199.6 15.9 %collective-permute-start = (bf16[1,8,16,768]{3,2,1,0:T(8,128)(2,1)S(1)}, bf16[1,8,16,768]{3,2,1,0:T(8,128)(2,1)S(1)}, u32[]{:S(2)}, u32[]{:S(2)}) collective-permute-start(bf16[1,8,16,768]{3,2,1,0:T(8,128)(2,1)S(1)} %get-tuple-element.1097), channel_id=1, source_target_pairs={{0,8},{8,16},{16,24},{1,9},{9,17},{17,25},{2,10},{10,18},{18,26},{... | collective-permute-start | bytes 589832 | tf_op jit(solution)/shard_map/while/body/eval_jaxpr/ppermute | solution.py:16
  215.6 16.6 %collective-permute-start.1 = (bf16[1,8,16,768]{3,2,1,0:T(8,128)(2,1)S(1)}, bf16[1,8,16,768]{3,2,1,0:T(8,128)(2,1)S(1)}, u32[]{:S(2)}, u32[]{:S(2)}) collective-permute-start(bf16[1,8,16,768]{3,2,1,0:T(8,128)(2,1)S(1)} %get-tuple-element.1098), channel_id=1, source_target_pairs={{8,0},{16,8},{24,16},{9,1},{17,9},{25,17},{10,2},{18,10},{26,18},{... | collective-permute-start | bytes 589832 | tf_op jit(solution)/shard_map/while/body/eval_jaxpr/ppermute | solution.py:16
  230.7 15.1 %collective-permute-start = (bf16[1,8,16,768]{3,2,1,0:T(8,128)(2,1)S(1)}, bf16[1,8,16,768]{3,2,1,0:T(8,128)(2,1)S(1)}, u32[]{:S(2)}, u32[]{:S(2)}) collective-permute-start(bf16[1,8,16,768]{3,2,1,0:T(8,128)(2,1)S(1)} %get-tuple-element.1097), channel_id=1, source_target_pairs={{0,8},{8,16},{16,24},{1,9},{9,17},{17,25},{2,10},{10,18},{18,26},{... | collective-permute-start | bytes 589832 | tf_op jit(solution)/shard_map/while/body/eval_jaxpr/ppermute | solution.py:16
  245.9 18.7 %collective-permute-start.1 = (bf16[1,8,16,768]{3,2,1,0:T(8,128)(2,1)S(1)}, bf16[1,8,16,768]{3,2,1,0:T(8,128)(2,1)S(1)}, u32[]{:S(2)}, u32[]{:S(2)}) collective-permute-start(bf16[1,8,16,768]{3,2,1,0:T(8,128)(2,1)S(1)} %get-tuple-element.1098), channel_id=1, source_target_pairs={{8,0},{16,8},{24,16},{9,1},{17,9},{25,17},{10,2},{18,10},{26,18},{... | collective-permute-start | bytes 589832 | tf_op jit(solution)/shard_map/while/body/eval_jaxpr/ppermute | solution.py:16
  263.1 7.6 %collective-permute-start = (bf16[1,8,16,768]{3,2,1,0:T(8,128)(2,1)S(1)}, bf16[1,8,16,768]{3,2,1,0:T(8,128)(2,1)S(1)}, u32[]{:S(2)}, u32[]{:S(2)}) collective-permute-start(bf16[1,8,16,768]{3,2,1,0:T(8,128)(2,1)S(1)} %get-tuple-element.1097), channel_id=1, source_target_pairs={{0,8},{8,16},{16,24},{1,9},{9,17},{17,25},{2,10},{10,18},{18,26},{... | collective-permute-start | bytes 589832 | tf_op jit(solution)/shard_map/while/body/eval_jaxpr/ppermute | solution.py:16
  (15 other events, 210.0 us)
Sparse Core Ops, SparseCore 0:
  9.0 32.6 all-gather.3
  43.3 38.3 all-gather.5
  83.3 49.9 all-gather.7
